TPU v7x, 32 devices: a whole 2x2x4 slice. The times are simulated.
32 devices in a mesh: dp: 8 (over z, x), tensor: 4 (over y, core).
Axes of the slice: x: 2, y: 2, z: 4, core: 2. Of those that a mesh axis runs over, the one named last changes fastest.
Arguments:
- tokens: bfloat16 [20480, 768], P(('dp', 'tensor')), may hold values from -6 to 6
- segment_ids: int32 [20480], P('dp'), may hold values from 0 to 8, as said below
- lengths: int32 [40], P('dp'), may hold values from 410 to 512, as said below
- w_query: bfloat16 [768, 768], P(None, 'tensor'), may hold values from -0.21875 to 0.21875
- b_query: float32 [768], P('tensor'), may hold values from -3 to 3
- w_key: bfloat16 [768, 768], P(None, 'tensor'), may hold values from -0.21875 to 0.21875
- w_value: bfloat16 [768, 768], P(None, 'tensor'), may hold values from -0.21875 to 0.21875
- b_value: float32 [768], P('tensor'), may hold values from -3 to 3
- w_output: bfloat16 [768, 768], P('tensor'), may hold values from -1.5 to 1.5
- b_output: float32 [768], replicated, may hold values from -2 to 2
- first_gain: float32 [768], replicated, may hold values from 0.5 to 1.5
- first_shift: float32 [768], replicated, may hold values from -2 to 2
- w_inner: bfloat16 [768, 3072], P(None, 'tensor'), may hold values from -0.21875 to 0.21875
- b_inner: float32 [3072], P('tensor'), may hold values from -3 to 3
- w_outer: bfloat16 [3072, 768], P('tensor'), may hold values from -0.109375 to 0.109375
- b_outer: float32 [768], replicated, may hold values from -2 to 2
- second_gain: float32 [768], replicated, may hold values from 0.5 to 1.5
- second_shift: float32 [768], replicated, may hold values from -2 to 2
- cotangent: bfloat16 [20480, 768], P(('dp', 'tensor')), may hold values from -6 to 6
Outputs:
- output: bfloat16 [20480, 768], P(('dp', 'tensor'))
- grad_tokens: bfloat16 [20480, 768], P(('dp', 'tensor'))
- grad_w_query: float32 [768, 768], P(None, 'tensor')
- grad_b_query: float32 [768], P('tensor')
- grad_w_key: float32 [768, 768], P(None, 'tensor')
- grad_w_value: float32 [768, 768], P(None, 'tensor')
- grad_b_value: float32 [768], P('tensor')
- grad_w_output: float32 [768, 768], P('tensor')
- grad_b_output: float32 [768], P('tensor')
- grad_first_gain: float32 [768], P('tensor')
- grad_first_shift: float32 [768], P('tensor')
- grad_w_inner: float32 [768, 3072], P(None, 'tensor')
- grad_b_inner: float32 [3072], P('tensor')
- grad_w_outer: float32 [3072, 768], P('tensor')
- grad_b_outer: float32 [768], P('tensor')
- grad_second_gain: float32 [768], P('tensor')
- grad_second_shift: float32 [768], P('tensor')
Inputs may be any that keep to these rules, and one draw needn't show every extreme that they name: `segment_ids`: along each packed sequence of 512 positions the ids start at 0, never fall, and rise by at most one a position; the first sequence reaches the largest id. `lengths`: live positions of each packed sequence; the first sequence is full.
All inputs are finite; a program needn't handle non-finite values.
Results may differ from a plain program's by a relative error of at most 0.019.
Values may be sent and summed in bfloat16 or wider, within the bound.
A program may use at most 128 MiB of HBM per device.

v0:
```python
import math
import jax
import jax.numpy as jnp
from jax import lax
from jax.sharding import PartitionSpec as P

HD = 64
LEN = 512
EPSILON = 1e-12
NEGATIVE = -1000000000.0


def normalize(value, gain, shift):
    average = jnp.mean(value, axis=-1, keepdims=True)
    centered = value - average
    variance = jnp.mean(centered * centered, axis=-1, keepdims=True)
    inverse = lax.rsqrt(variance + EPSILON)
    unit = centered * inverse
    return (unit * gain + shift, unit, inverse)


def norm_backward(grad, unit, inverse, gain):
    scaled = grad * gain
    first_mean = jnp.mean(scaled, axis=-1, keepdims=True)
    second_mean = jnp.mean(scaled * unit, axis=-1, keepdims=True)
    result = inverse * (scaled - first_mean - unit * second_mean)
    return (result, jnp.sum(grad * unit, axis=0), jnp.sum(grad, axis=0))


def gelu_value(inner):
    return 0.5 * inner * (1.0 + lax.erf(inner * (1.0 / math.sqrt(2.0))))


def gelu_slope(inner):
    cumulative = 0.5 * (1.0 + lax.erf(inner * (1.0 / math.sqrt(2.0))))
    return cumulative + inner * jnp.exp(-0.5 * inner * inner) * (1.0 / math.sqrt(2.0 * math.pi))


def allowed_mask(segments, length):
    places = jnp.arange(segments.shape[0])
    same = segments[:, None] == segments[None, :]
    live = places[None, :] < length
    return same & live | (places[:, None] == places[None, :])


def split_heads(rows):
    return rows.reshape(rows.shape[0], rows.shape[1] // HD, HD)


def attention_logits(query_rows, key_rows, segments, length):
    scores = jnp.einsum(
        "qhd,khd->hqk",
        split_heads(query_rows),
        split_heads(key_rows),
        preferred_element_type=jnp.float32,
    )
    return jnp.where(allowed_mask(segments, length)[None], scores * (1.0 / math.sqrt(HD)), NEGATIVE)


def forward_attend(block):
    query_rows, key_rows, value_rows, segments, length = block
    logits = attention_logits(query_rows, key_rows, segments, length)
    peak = jnp.max(logits, axis=-1, keepdims=True)
    powers = jnp.exp(logits - peak)
    total = jnp.sum(powers, axis=-1, keepdims=True)
    weights = (powers / total).astype(jnp.bfloat16)
    context = jnp.einsum(
        "hqk,khd->qhd", weights, split_heads(value_rows), preferred_element_type=jnp.float32
    )
    log_total = (peak + jnp.log(total))[..., 0]
    return (context.reshape(query_rows.shape).astype(jnp.bfloat16), log_total)


def backward_attend(block):
    query_rows, key_rows, value_rows, grad_rows, segments, length, log_total = block
    logits = attention_logits(query_rows, key_rows, segments, length)
    probs = jnp.exp(logits - log_total[..., None])
    grad_heads = split_heads(grad_rows)
    grad_probs = jnp.einsum(
        "qhd,khd->hqk", grad_heads, split_heads(value_rows), preferred_element_type=jnp.float32
    )
    across = jnp.sum(probs * grad_probs, axis=-1, keepdims=True)
    grad_scores = (probs * (grad_probs - across) * (1.0 / math.sqrt(HD))).astype(jnp.bfloat16)
    grad_query = jnp.einsum(
        "hqk,khd->qhd", grad_scores, split_heads(key_rows), preferred_element_type=jnp.float32
    )
    grad_key = jnp.einsum(
        "hqk,qhd->khd", grad_scores, split_heads(query_rows), preferred_element_type=jnp.float32
    )
    grad_value = jnp.einsum(
        "hqk,qhd->khd", probs.astype(jnp.bfloat16), grad_heads, preferred_element_type=jnp.float32
    )
    shape = query_rows.shape
    joined = jnp.concatenate(
        [grad_query.reshape(shape), grad_key.reshape(shape), grad_value.reshape(shape)], axis=1
    )
    return joined.astype(jnp.bfloat16)


def shards(
    tokens,
    segment_ids,
    lengths,
    w_query,
    b_query,
    w_key,
    w_value,
    b_value,
    w_output,
    b_output,
    first_gain,
    first_shift,
    w_inner,
    b_inner,
    w_outer,
    b_outer,
    second_gain,
    second_shift,
    cotangent,
):
    parts = lax.axis_size("tensor")
    width = w_query.shape[1]
    count = segment_ids.shape[0] // LEN
    joined = jnp.concatenate([w_query, w_key, w_value], axis=1)

    def by_sequence(rows_all):
        return rows_all.reshape(count, LEN, rows_all.shape[1])

    whole = lax.all_gather(tokens, "tensor", axis=0, tiled=True)
    projected = jnp.dot(whole, joined, preferred_element_type=jnp.float32)
    query_rows = (projected[:, :width] + b_query).astype(jnp.bfloat16)
    key_rows = projected[:, width : 2 * width].astype(jnp.bfloat16)
    value_rows = (projected[:, 2 * width :] + b_value).astype(jnp.bfloat16)
    segments = segment_ids.reshape(count, LEN)
    context, log_total = lax.map(
        forward_attend,
        (
            by_sequence(query_rows),
            by_sequence(key_rows),
            by_sequence(value_rows),
            segments,
            lengths,
        ),
    )
    context = context.reshape(count * LEN, width)
    piece = context
    attended = lax.psum_scatter(
        jnp.dot(piece, w_output, preferred_element_type=jnp.float32),
        "tensor",
        scatter_dimension=0,
        tiled=True,
    )
    first_full, first_unit, first_inverse = normalize(
        tokens.astype(jnp.float32) + attended + b_output, first_gain, first_shift
    )
    first_out = first_full.astype(jnp.bfloat16)
    ffn_rows = lax.all_gather(first_out, "tensor", axis=0, tiled=True)
    inner = jnp.dot(ffn_rows, w_inner, preferred_element_type=jnp.float32) + b_inner
    hidden = gelu_value(inner).astype(jnp.bfloat16)
    piece = hidden
    feed_out = lax.psum_scatter(
        jnp.dot(piece, w_outer, preferred_element_type=jnp.float32).astype(jnp.bfloat16),
        "tensor",
        scatter_dimension=0,
        tiled=True,
    ).astype(jnp.float32)
    second_full, second_unit, second_inverse = normalize(
        first_out.astype(jnp.float32) + feed_out + b_outer, second_gain, second_shift
    )
    output = second_full.astype(jnp.bfloat16)
    grad_second, grad_second_gain, grad_second_shift = norm_backward(
        cotangent.astype(jnp.float32), second_unit, second_inverse, second_gain
    )
    grad_feed = grad_second.astype(jnp.bfloat16)
    grad_b_outer = jnp.sum(grad_feed.astype(jnp.float32), axis=0)
    feed_grads = lax.all_gather(grad_feed, "tensor", axis=0, tiled=True)
    grad_w_outer = jnp.einsum("gf,gd->fd", hidden, feed_grads, preferred_element_type=jnp.float32)
    grad_hidden = jnp.einsum("gd,fd->gf", feed_grads, w_outer, preferred_element_type=jnp.float32)
    grad_inner = (grad_hidden * gelu_slope(inner)).astype(jnp.bfloat16)
    grad_b_inner = jnp.sum(grad_inner.astype(jnp.float32), axis=0)
    grad_w_inner = jnp.einsum("gd,gf->df", ffn_rows, grad_inner, preferred_element_type=jnp.float32)
    piece = grad_inner
    grad_first = grad_second + lax.psum_scatter(
        jnp.einsum("gf,df->gd", piece, w_inner, preferred_element_type=jnp.float32).astype(
            jnp.bfloat16
        ),
        "tensor",
        scatter_dimension=0,
        tiled=True,
    ).astype(jnp.float32)
    grad_branch_full, grad_first_gain, grad_first_shift = norm_backward(
        grad_first, first_unit, first_inverse, first_gain
    )
    grad_branch = grad_branch_full.astype(jnp.bfloat16)
    grad_b_output = jnp.sum(grad_branch.astype(jnp.float32), axis=0)
    branch_rows = lax.all_gather(grad_branch, "tensor", axis=0, tiled=True)
    grad_w_output = jnp.einsum(
        "gc,gd->cd", context, branch_rows, preferred_element_type=jnp.float32
    )
    grad_context = jnp.einsum(
        "gd,cd->gc", branch_rows, w_output, preferred_element_type=jnp.float32
    ).astype(jnp.bfloat16)
    grad_joined = lax.map(
        backward_attend,
        (
            by_sequence(query_rows),
            by_sequence(key_rows),
            by_sequence(value_rows),
            by_sequence(grad_context),
            segments,
            lengths,
            log_total,
        ),
    )
    grad_joined = grad_joined.reshape(count * LEN, 3 * width)
    grad_w_joined = jnp.einsum("gd,gc->dc", whole, grad_joined, preferred_element_type=jnp.float32)
    grad_bias_all = jnp.sum(grad_joined.astype(jnp.float32), axis=0)
    grad_b_query = grad_bias_all[:width]
    grad_b_value = grad_bias_all[2 * width :]
    input_terms = jnp.einsum("gc,dc->gd", grad_joined, joined, preferred_element_type=jnp.float32)
    small = jnp.stack(
        [
            grad_b_output,
            grad_first_gain,
            grad_first_shift,
            grad_b_outer,
            grad_second_gain,
            grad_second_shift,
        ]
    )
    small_flat = small.reshape(6, parts, small.shape[1] // parts).transpose(1, 0, 2).reshape(-1)
    input_share, small_share = (
        lax.psum_scatter(
            input_terms.astype(jnp.bfloat16), "tensor", scatter_dimension=0, tiled=True
        ).astype(jnp.float32),
        lax.psum_scatter(
            small_flat.astype(jnp.bfloat16), "tensor", scatter_dimension=0, tiled=True
        ).astype(jnp.float32),
    )
    grad_tokens = (grad_branch_full + input_share).astype(jnp.bfloat16)
    small_share = small_share.reshape(6, small_share.shape[0] // 6)
    (
        grad_w_joined,
        grad_b_query,
        grad_b_value,
        grad_w_output,
        grad_w_inner,
        grad_b_inner,
        grad_w_outer,
        small_share,
    ) = lax.psum(
        (
            grad_w_joined,
            grad_b_query,
            grad_b_value,
            grad_w_output,
            grad_w_inner,
            grad_b_inner,
            grad_w_outer,
            small_share,
        ),
        "dp",
    )
    return (
        output,
        grad_tokens,
        grad_w_joined[:, :width],
        grad_b_query,
        grad_w_joined[:, width : 2 * width],
        grad_w_joined[:, 2 * width :],
        grad_b_value,
        grad_w_output,
        small_share[0],
        small_share[1],
        small_share[2],
        grad_w_inner,
        grad_b_inner,
        grad_w_outer,
        small_share[3],
        small_share[4],
        small_share[5],
    )


def solution(mesh):
    in_specs = (
        P(("dp", "tensor"), None),
        P("dp"),
        P("dp"),
        P(None, "tensor"),
        P("tensor"),
        P(None, "tensor"),
        P(None, "tensor"),
        P("tensor"),
        P("tensor", None),
        P(),
        P(),
        P(),
        P(None, "tensor"),
        P("tensor"),
        P("tensor", None),
        P(),
        P(),
        P(),
        P(("dp", "tensor"), None),
    )
    out_specs = (
        P(("dp", "tensor"), None),
        P(("dp", "tensor"), None),
        P(None, "tensor"),
        P("tensor"),
        P(None, "tensor"),
        P(None, "tensor"),
        P("tensor"),
        P("tensor", None),
        P("tensor"),
        P("tensor"),
        P("tensor"),
        P(None, "tensor"),
        P("tensor"),
        P("tensor", None),
        P("tensor"),
        P("tensor"),
        P("tensor"),
    )
    return jax.shard_map(shards, mesh=mesh, in_specs=in_specs, out_specs=out_specs, check_vma=False)
```

profile of v0, /device:TPU:0, one launch (start us, length us, event | category | flops | bytes accessed | tf_op | source)
XLA Modules:
  0.0 826.7 jit_solution(1804968826815909880)
XLA Ops:
  10.7 34.6 %all-gather.5.cloned.1.call-done = bf16[2560,768]{1,0:T(8,128)(2,1)} async-done(((bf16[640,768]{1,0:T(8,128)(2,1)}), bf16[2560,768]{1,0:T(8,128)(2,1)}) %all-gather.5.cloned.1.call-update) | async-done | bytes 3932176 | tf_op jit(solution)/shard_map/all_gather | solution.py:129
  45.3 4.6 convolution_bitcast_fusion
  60.1 37.0 %while.22 = (s32[]{:T(128)}, bf16[5,512,192]{1,2,0:T(8,128)(2,1)S(1)}, f32[5,3,512]{2,1,0:T(4,128)}, bf16[5,512,192]{1,2,0:T(8,128)(2,1)}, s32[5,512]{1,0:T(8,12...) while((s32[]{:T(128)}, ...), condition=%wide.region_3.4_spmd, body=%wide.region_0.3_spmd.sunk | while | flops 211909632 | bytes 12903561 | solution.py:135
  97.7 5.4 fusion.60
  103.2 69.1 %reduce-scatter.5.cloned.1.call-done = f32[640,768]{1,0:T(8,128)} async-done(((f32[2560,768]{1,0:T(8,128)}), f32[640,768]{1,0:T(8,128)}) %reduce-scatter.5.cloned.1.call-update) | async-done | bytes 1966096 | tf_op jit(solution)/shard_map/reduce_scatter | solution.py:147
  177.0 32.6 %all-gather.7.cloned.1.call-done = bf16[2560,768]{1,0:T(8,128)(2,1)} async-done(((bf16[640,768]{1,0:T(8,128)(2,1)}), bf16[2560,768]{1,0:T(8,128)(2,1)}) %all-gather.7.cloned.1.call-update) | async-done | bytes 3932176 | tf_op jit(solution)/shard_map/all_gather | solution.py:157
  209.6 7.5 multiply_convert_fusion.1
  219.0 4.7 convolution_convert_fusion.1
  223.8 43.0 %reduce-scatter.7.cloned.1.call-done = bf16[640,768]{1,0:T(8,128)(2,1)} async-done(((bf16[2560,768]{1,0:T(8,128)(2,1)}), bf16[640,768]{1,0:T(8,128)(2,1)}) %reduce-scatter.7.cloned.1.call-update) | async-done | bytes 983056 | tf_op jit(solution)/shard_map/reduce_scatter | solution.py:161
  276.5 33.1 %all-gather.9.cloned.1.call-done = bf16[2560,768]{1,0:T(8,128)(2,1)} async-done(((bf16[640,768]{1,0:T(8,128)(2,1)}), bf16[2560,768]{1,0:T(8,128)(2,1)}) %all-gather.9.cloned.1.call-update) | async-done | bytes 3932176 | tf_op jit(solution)/shard_map/all_gather | solution.py:176
  309.6 9.6 %convert_reduce_fusion = (f32[768]{0:T(1024)}, bf16[2560,768]{1,0:T(8,128)(2,1)S(1)}) fusion(f32[2560,768]{1,0:T(8,128)} %get-tuple-element.259, f32[768]{0:T(1024)S(1)} %copy-done.37, bf16[2560,768]{1,0:T(8,128)(2,1)} %all-gather.9.cloned.1.call-done, bf16[768,768]{1,0:T(8,128)(2,1)} %param.37), kind=kOutput, calls=%fused_computation.53 | convolution fusion | flops 3045457152 | bytes 16914432 | tf_op jit(solution)/shard_map/gd,fd->gf/dot_general | solution.py:178
  321.1 4.8 convolution_convert_fusion
  326.1 42.8 %reduce-scatter.9.cloned.1.call-done = bf16[640,768]{1,0:T(8,128)(2,1)} async-done(((bf16[2560,768]{1,0:T(8,128)(2,1)}), bf16[640,768]{1,0:T(8,128)(2,1)}) %reduce-scatter.9.cloned.1.call-update) | async-done | bytes 983056 | tf_op jit(solution)/shard_map/reduce_scatter | solution.py:183
  375.4 8.1 fusion.63
  383.6 4.8 fusion.62
  388.4 20.1 %all-gather.11.cloned.1.call-done = bf16[2560,768]{1,0:T(8,128)(2,1)} async-done(((bf16[640,768]{1,0:T(8,128)(2,1)}), bf16[2560,768]{1,0:T(8,128)(2,1)}) %all-gather.11.cloned.1.call-update) | async-done | bytes 3932176 | tf_op jit(solution)/shard_map/all_gather | solution.py:196
  414.2 102.7 %while.23 = (s32[]{:T(128)}, bf16[5,512,576]{1,2,0:T(8,128)(2,1)}, bf16[5,512,192]{1,2,0:T(8,128)(2,1)}, s32[5,512]{1,0:T(8,128)S(1)}, s32[5]{0:T(128)}, /*index...) while((s32[]{:T(128)}, bf16[5,512,576]{1,2,0:T(8,128)(2,1)}, ...), condition=%wide.region_17.18_spmd, body=%wide.region_15.17_spmd.sunk | while | flops 517444096 | bytes 28075180 | solution.py:203
  423.8 4.7 fusion.141
  428.4 4.4 fusion.140
  444.3 4.7 fusion.141
  464.8 4.7 fusion.141
  469.5 4.4 fusion.140
  485.4 4.7 fusion.141
  506.0 4.7 fusion.141
  510.6 4.4 fusion.140
  516.9 4.8 copy.98
  525.8 6.0 convolution_bitcast_fusion.1
  533.7 5.8 convolution_convert_fusion.2
  542.1 11.0 %all-reduce = bf16[4608]{0:T(1024)(128)(2,1)S(1)} all-reduce(bf16[4608]{0:T(1024)(128)(2,1)S(1)} %convert_element_type.135), channel_id=6, replica_groups=mesh['dp'=8,'tensor'=4] {'tensor'}, use_global_device_ids=true, to_apply=%region_30.31.clone | all-reduce | flops 4608 | bytes 18432
  553.7 40.0 %all-reduce.1 = (f32[192]{0:T(256)}, f32[192]{0:T(256)}, f32[6,192]{1,0:T(8,128)S(1)}, f32[768]{0:T(1024)}) all-reduce(f32[192]{0:T(256)S(1)} %get-tuple-element.257, f32[192]{0:T(256)S(1)} %get-tuple-element.256, f32[6,192]{1,0:T(8,128)S(1)} %reshape.391, f32[768]{0:T(1024)S(1)} %copy-done.31), channel_id=1, replica_groups=mesh['dp'=8,'tensor'=4] {'dp'}, use_global_device_ids=true, to_apply=%region_21.22 | all-reduce | flops 2304 | bytes 18432 | tf_op jit(solution)/shard_map/psum | solution.py:251
  594.3 174.0 %all-reduce.5.cloned.1.call-done = (f32[768,576]{0,1:T(8,128)}, f32[192,768]{1,0:T(8,128)}, f32[768,768]{1,0:T(8,128)}, f32[768,768]{1,0:T(8,128)}) async-done(((f32[768,576]{0,1:T(8,128)}, f32[192,768]{1,0:T(8,128)}, f32[768,768]{1,0:T(8,128)}, f32[768,768]{1,0:T(8,128)}), (f32[768,576]{0,1:T(8,128)}, f32[192,768]{1,0:T(8,128)}, f32[768,768]{1,0:T(8,128)}, ...) | async-done | bytes 7077904 | tf_op jit(solution)/shard_map/psum | solution.py:251
  770.9 41.8 %reduce-scatter.11.cloned.1.call-done = bf16[640,768]{1,0:T(8,128)(2,1)} async-done(((bf16[2560,768]{1,0:T(8,128)(2,1)}), bf16[640,768]{1,0:T(8,128)(2,1)}) %reduce-scatter.11.cloned.1.call-update) | async-done | bytes 983056 | tf_op jit(solution)/shard_map/reduce_scatter | solution.py:233
  (283 shorter events, 166.3 us)
Async XLA Ops:
  7.2 202.4 %copy-start = (bf16[768,768]{1,0:T(8,128)(2,1)S(1)}, bf16[768,768]{1,0:T(8,128)(2,1)}, u32[]{:S(2)}) copy-start(bf16[768,768]{1,0:T(8,128)(2,1)} %param.35) | copy-start | bytes 3538948
  7.2 3.5 copy-start.18
  7.2 38.1 %all-gather.5.cloned.1.call-start = ((), (), s32[]{:S(2)}) async-start(), calls=%async_computation.4 | async-start | bytes 4915200 | tf_op jit(solution)/shard_map/all_gather | solution.py:129
  7.9 164.3 %reduce-scatter.5.cloned.1.call-start = ((), (), s32[]{:S(2)}) async-start(), calls=%async_computation.5 | async-start | bytes 9830400 | tf_op jit(solution)/shard_map/reduce_scatter | solution.py:147
  10.7 39.2 %copy-start.21 = (bf16[768,576]{0,1:T(8,128)(2,1)}, bf16[768,576]{0,1:T(8,128)(2,1)S(1)}, u32[]{:S(2)}) copy-start(bf16[768,576]{0,1:T(8,128)(2,1)S(1)} %constant_dynamic-update-slice_fusion.1) | copy-start | bytes 2654212
  97.7 5.4 copy-start.6
  103.1 69.2 %copy-start.30 = (f32[768]{0:T(1024)S(1)}, f32[768]{0:T(1024)}, u32[]{:S(2)}) copy-start(f32[768]{0:T(1024)} %param.32) | copy-start | bytes 9220
  103.1 106.5 %all-gather.7.cloned.1.call-start = ((), (), s32[]{:S(2)}) async-start(), calls=%async_computation.6 | async-start | bytes 4915200 | tf_op jit(solution)/shard_map/all_gather | solution.py:157
  175.1 34.5 %copy-start.37 = (f32[768]{0:T(1024)S(1)}, f32[768]{0:T(1024)}, u32[]{:S(2)}) copy-start(f32[768]{0:T(1024)} %param.36) | copy-start | bytes 9220
  176.5 90.3 %reduce-scatter.7.cloned.1.call-start = ((), (), s32[]{:S(2)}) async-start(), calls=%async_computation.7 | async-start | bytes 4915200 | tf_op jit(solution)/shard_map/reduce_scatter | solution.py:161
  209.6 9.4 %copy-start.36 = (bf16[768,768]{1,0:T(8,128)(2,1)S(1)}, bf16[768,768]{1,0:T(8,128)(2,1)}, u32[]{:S(2)}) copy-start(bf16[768,768]{1,0:T(8,128)(2,1)} %param.37) | copy-start | bytes 3538948
  223.7 43.1 %copy-start.22 = (f32[768]{0:T(1024)S(1)}, f32[768]{0:T(1024)}, u32[]{:S(2)}) copy-start(f32[768]{0:T(1024)} %param.38) | copy-start | bytes 9220
  223.8 85.9 %all-gather.9.cloned.1.call-start = ((), (), s32[]{:S(2)}) async-start(), calls=%async_computation.8 | async-start | bytes 4915200 | tf_op jit(solution)/shard_map/all_gather | solution.py:176
  276.5 92.5 %reduce-scatter.9.cloned.1.call-start = ((), (), s32[]{:S(2)}) async-start(), calls=%async_computation.9 | async-start | bytes 4915200 | tf_op jit(solution)/shard_map/reduce_scatter | solution.py:183
  325.9 82.6 %all-gather.11.cloned.1.call-start = ((), (), s32[]{:S(2)}) async-start(), calls=%async_computation.10 | async-start | bytes 4915200 | tf_op jit(solution)/shard_map/all_gather | solution.py:196
  369.0 3.5 copy-start.2
  369.0 3.5 copy-start.9
  375.4 392.9 %all-reduce.5.cloned.1.call-start = ((), (), s32[]{:S(2)}) async-start(), calls=%async_computation.12 | async-start | bytes 14155776 | tf_op jit(solution)/shard_map/psum | solution.py:251
  375.4 8.2 copy-start.35
  375.4 8.2 copy-start.41
  383.6 24.9 %copy-start.17 = (bf16[192,768]{1,0:T(8,128)(2,1)S(1)}, bf16[192,768]{1,0:T(8,128)(2,1)}, u32[]{:S(2)}) copy-start(bf16[192,768]{1,0:T(8,128)(2,1)} %param.31) | copy-start | bytes 884740
  516.9 4.8 copy-start.7
  521.7 4.0 copy-start.11
  531.8 280.9 %reduce-scatter.11.cloned.1.call-start = ((), (), s32[]{:S(2)}) async-start(), calls=%async_computation.11 | async-start | bytes 4915200 | tf_op jit(solution)/shard_map/reduce_scatter | solution.py:233
  539.5 2.3 copy-start.29
  539.6 13.7 %copy-start.4 = (bf16[5,512,576]{1,2,0:T(8,128)(2,1)S(1)}, bf16[5,512,576]{1,2,0:T(8,128)(2,1)}, u32[]{:S(2)}) copy-start(bf16[5,512,576]{1,2,0:T(8,128)(2,1)} %get-tuple-element.109) | copy-start | bytes 8847364
  539.6 14.1 %copy-start.31 = (f32[768]{0:T(1024)S(1)}, f32[768]{0:T(1024)}, u32[]{:S(2)}) copy-start(f32[768]{0:T(1024)} %get-tuple-element.260) | copy-start | bytes 9220
  553.7 259.0 %copy-start.5 = (f32[640,768]{1,0:T(8,128)S(1)}, f32[640,768]{1,0:T(8,128)}, u32[]{:S(2)}) copy-start(f32[640,768]{1,0:T(8,128)} %get-tuple-element.232) | copy-start | bytes 5898244
  812.7 2.5 copy-start.16
  812.7 3.3 copy-start.14
  816.1 2.5 copy-start.13
  816.1 3.9 copy-start.1
  (23 other events, 30.7 us)
Sparse Core Ops, SparseCore 0:
  9.6 35.6 all-gather.4
  103.2 68.9 reduce-scatter.4
  176.6 32.9 all-gather.6
  223.9 42.8 reduce-scatter.6
  276.6 32.9 all-gather.8
  326.0 42.8 reduce-scatter.8
  375.5 32.9 all-gather.10
  531.9 236.3 all-reduce.4
  770.8 41.8 reduce-scatter.10
where the time goes:
time: 835 us; the launch traced here: 827 us
  waiting for transfers between devices  492 us (59%)
  matrix products  143 us (17%)
  local copies, waits for them, and re-layouts  75.5 us (9%)
  blocking collectives  50.9 us (6%)
  other arithmetic  48.9 us (6%)
  between operations  15.1 us (2%)
    psum x1, waiting for transfers between devices, shards(): lax.psum((grad_w_joined, grad_b_query, grad_b_value, grad_w_output, grad_...  174 us
    reduce_scatter x1, waiting for transfers between devices, shards(): lax.psum_scatter(jnp.dot(piece, w_output, preferred_element_type=jnp.floa...  69.1 us
    reduce_scatter x1, waiting for transfers between devices, shards(): lax.psum_scatter(jnp.dot(piece, w_outer, preferred_element_type=jnp.float...  43 us
    reduce_scatter x1, waiting for transfers between devices, shards(): lax.psum_scatter(jnp.einsum('gf,df->gd', piece, w_inner, preferred_elemen...  42.8 us
    reduce_scatter x1, waiting for transfers between devices, shards(): lax.psum_scatter(input_terms.astype(jnp.bfloat16), 'tensor', scatter_dime...  41.8 us
    psum x1, blocking collectives, shards(): lax.psum((grad_w_joined, grad_b_query, grad_b_value, grad_w_output, grad_...  40 us
    all_gather x1, waiting for transfers between devices, shards(): whole = lax.all_gather(tokens, 'tensor', axis=0, tiled=True)  34.6 us
    all_gather x1, waiting for transfers between devices, shards(): feed_grads = lax.all_gather(grad_feed, 'tensor', axis=0, tiled=True)  33.1 us
  transfers between devices with their start and end apart: 9, of which 9 were waited for; matrix products, arithmetic and copies ran while one was open for 3% of the time, Pallas kernels for 0%

commit v1 on v0

--- a/solution.py
+++ b/solution.py
@@ -154,7 +154,15 @@
         tokens.astype(jnp.float32) + attended + b_output, first_gain, first_shift
     )
     first_out = first_full.astype(jnp.bfloat16)
-    ffn_rows = lax.all_gather(first_out, "tensor", axis=0, tiled=True)
+    ways, here, step = (lax.axis_size("tensor"), lax.axis_index("tensor"), first_out.shape[0])
+    line, have = (first_out, 1)
+    while have < ways:
+        line = jnp.concatenate(
+            [line, lax.ppermute(line, "tensor", [(d, (d - have) % ways) for d in range(ways)])],
+            axis=0,
+        )
+        have = 2 * have
+    ffn_rows = jnp.roll(line, here * step, axis=0)
     inner = jnp.dot(ffn_rows, w_inner, preferred_element_type=jnp.float32) + b_inner
     hidden = gelu_value(inner).astype(jnp.bfloat16)
     piece = hidden

time: 835 us -> 879 us (1.053)
  waiting for transfers between devices: 492 us -> 513 us
  local copies, waits for them, and re-layouts: 75.5 us -> 91.5 us
    ppermute x0 -> x2, waiting for transfers between devices: none -> 53.6 us  [shards(): lax.ppermute(line, 'tensor', [(d, (d - have) % ways) for d in range(ways)])]
    all_gather x1 -> x0, waiting for transfers between devices: 32.6 us -> none  [shards(): ffn_rows = lax.all_gather(first_out, 'tensor', axis=0, tiled=True)]
    unnamed x93 -> x97, local copies, waits for them, and re-layouts: 14.3 us -> 22.1 us
  transfers between devices with their start and end apart: 9 -> 10, of which waited for: 9 -> 10; matrix products, arithmetic and copies ran while one was open for 3% -> 3% of each run, Pallas kernels for 0% -> 0%
where the time goes in v1:
time: 879 us; the launch traced here: 870 us
  waiting for transfers between devices  513 us (58%)
  matrix products  142 us (16%)
  local copies, waits for them, and re-layouts  91.5 us (10%)
  other arithmetic  54.3 us (6%)
  blocking collectives  51 us (6%)
  between operations  15.4 us (2%)
    psum x1, waiting for transfers between devices, shards(): lax.psum((grad_w_joined, grad_b_query, grad_b_value, grad_w_output, grad_...  174 us
    reduce_scatter x1, waiting for transfers between devices, shards(): lax.psum_scatter(jnp.dot(piece, w_output, preferred_element_type=jnp.floa...  69.1 us
    ppermute x2, waiting for transfers between devices, shards(): lax.ppermute(line, 'tensor', [(d, (d - have) % ways) for d in range(ways)])  53.6 us
    reduce_scatter x1, waiting for transfers between devices, shards(): lax.psum_scatter(jnp.dot(piece, w_outer, preferred_element_type=jnp.float...  44.2 us
    reduce_scatter x1, waiting for transfers between devices, shards(): lax.psum_scatter(jnp.einsum('gf,df->gd', piece, w_inner, preferred_elemen...  42.8 us
    reduce_scatter x1, waiting for transfers between devices, shards(): lax.psum_scatter(input_terms.astype(jnp.bfloat16), 'tensor', scatter_dime...  41.7 us
    psum x1, blocking collectives, shards(): lax.psum((grad_w_joined, grad_b_query, grad_b_value, grad_w_output, grad_...  40 us
    all_gather x1, waiting for transfers between devices, shards(): whole = lax.all_gather(tokens, 'tensor', axis=0, tiled=True)  33.6 us
  transfers between devices with their start and end apart: 10, of which 10 were waited for; matrix products, arithmetic and copies ran while one was open for 3% of the time, Pallas kernels for 0%

profile of v1, /device:TPU:0, one launch (start us, length us, event | category | flops | bytes accessed | tf_op | source)
XLA Modules:
  0.0 870.3 jit_solution(7133655208353532817)
XLA Ops:
  11.7 33.6 %all-gather.4.cloned.1.call-done = bf16[2560,768]{1,0:T(8,128)(2,1)} async-done(((bf16[640,768]{1,0:T(8,128)(2,1)}), bf16[2560,768]{1,0:T(8,128)(2,1)}) %all-gather.4.cloned.1.call-update) | async-done | bytes 3932176 | tf_op jit(solution)/shard_map/all_gather | solution.py:129
  45.3 4.6 convolution_bitcast_fusion
  60.1 40.3 %while.22 = (s32[]{:T(128)}, bf16[5,512,192]{1,2,0:T(8,128)(2,1)}, f32[5,3,512]{2,1,0:T(4,128)}, bf16[5,512,192]{1,2,0:T(8,128)(2,1)}, s32[5,512]{1,0:T(8,128)S(...) while((s32[]{:T(128)}, bf16[5,512,192]{1,2,0:T(8,128)(2,1)}, ...), condition=%wide.region_3.4_spmd, body=%wide.region_0.3_spmd.sunk | while | flops 211909632 | bytes 12903561 | solution.py:135
  106.2 69.1 %reduce-scatter.5.cloned.1.call-done = f32[640,768]{1,0:T(8,128)} async-done(((f32[2560,768]{1,0:T(8,128)}), f32[640,768]{1,0:T(8,128)}) %reduce-scatter.5.cloned.1.call-update) | async-done | bytes 1966096 | tf_op jit(solution)/shard_map/reduce_scatter | solution.py:147
  180.1 11.9 %collective-permute-done = bf16[640,768]{1,0:T(8,128)(2,1)S(1)} collective-permute-done((bf16[640,768]{1,0:T(8,128)(2,1)}, bf16[640,768]{1,0:T(8,128)(2,1)S(1)}, u32[]{:S(2)}, u32[]{:S(2)}) %collective-permute-start) | collective-permute-done | bytes 983072 | tf_op jit(solution)/shard_map/ppermute | solution.py:161
  199.2 41.7 %collective-permute-done.1 = bf16[1280,768]{1,0:T(8,128)(2,1)} collective-permute-done((bf16[1280,768]{1,0:T(8,128)(2,1)}, bf16[1280,768]{1,0:T(8,128)(2,1)}, u32[]{:S(2)}, u32[]{:S(2)}) %collective-permute-start.1) | collective-permute-done | bytes 1966112 | tf_op jit(solution)/shard_map/ppermute | solution.py:161
  250.1 7.9 multiply_convert_fusion.1
  259.9 4.8 convolution_convert_fusion.1
  264.8 44.2 %reduce-scatter.7.cloned.1.call-done = bf16[640,768]{1,0:T(8,128)(2,1)} async-done(((bf16[2560,768]{1,0:T(8,128)(2,1)}), bf16[640,768]{1,0:T(8,128)(2,1)}) %reduce-scatter.7.cloned.1.call-update) | async-done | bytes 983056 | tf_op jit(solution)/shard_map/reduce_scatter | solution.py:169
  320.9 33.1 %all-gather.6.cloned.1.call-done = bf16[2560,768]{1,0:T(8,128)(2,1)} async-done(((bf16[640,768]{1,0:T(8,128)(2,1)}), bf16[2560,768]{1,0:T(8,128)(2,1)}) %all-gather.6.cloned.1.call-update) | async-done | bytes 3932176 | tf_op jit(solution)/shard_map/all_gather | solution.py:184
  354.0 9.6 %convert_reduce_fusion = (f32[768]{0:T(1024)}, bf16[2560,768]{1,0:T(8,128)(2,1)S(1)}) fusion(f32[2560,768]{1,0:T(8,128)} %get-tuple-element.261, f32[768]{0:T(1024)S(1)} %copy-done.37, bf16[2560,768]{1,0:T(8,128)(2,1)} %all-gather.6.cloned.1.call-done, bf16[768,768]{1,0:T(8,128)(2,1)} %param.37), kind=kOutput, calls=%fused_computation.53 | convolution fusion | flops 3045457152 | bytes 16914432 | tf_op jit(solution)/shard_map/gd,fd->gf/dot_general | solution.py:186
  365.5 4.8 convolution_convert_fusion
  370.5 42.8 %reduce-scatter.9.cloned.1.call-done = bf16[640,768]{1,0:T(8,128)(2,1)} async-done(((bf16[2560,768]{1,0:T(8,128)(2,1)}), bf16[640,768]{1,0:T(8,128)(2,1)}) %reduce-scatter.9.cloned.1.call-update) | async-done | bytes 983056 | tf_op jit(solution)/shard_map/reduce_scatter | solution.py:191
  419.8 8.2 fusion.41
  427.9 4.8 fusion.68
  432.7 20.2 %all-gather.8.cloned.1.call-done = bf16[2560,768]{1,0:T(8,128)(2,1)} async-done(((bf16[640,768]{1,0:T(8,128)(2,1)}), bf16[2560,768]{1,0:T(8,128)(2,1)}) %all-gather.8.cloned.1.call-update) | async-done | bytes 3932176 | tf_op jit(solution)/shard_map/all_gather | solution.py:204
  458.6 102.6 %while.23 = (s32[]{:T(128)}, bf16[5,512,576]{1,2,0:T(8,128)(2,1)}, bf16[5,512,192]{1,2,0:T(8,128)(2,1)}, s32[5,512]{1,0:T(8,128)S(1)}, s32[5]{0:T(128)}, /*index...) while((s32[]{:T(128)}, bf16[5,512,576]{1,2,0:T(8,128)(2,1)}, ...), condition=%wide.region_17.18_spmd, body=%wide.region_15.17_spmd.sunk | while | flops 517444096 | bytes 28075180 | solution.py:211
  468.1 4.7 fusion.144
  488.7 4.7 fusion.144
  493.3 4.4 fusion.143
  509.2 4.7 fusion.144
  529.7 4.7 fusion.144
  534.3 4.4 fusion.143
  550.2 4.7 fusion.144
  554.9 4.4 fusion.143
  561.2 4.8 copy.98
  570.1 6.0 convolution_bitcast_fusion.1
  578.0 5.8 convolution_convert_fusion.2
  586.4 11.0 %all-reduce = bf16[4608]{0:T(1024)(128)(2,1)S(1)} all-reduce(bf16[4608]{0:T(1024)(128)(2,1)S(1)} %convert_element_type.135), channel_id=6, replica_groups=mesh['dp'=8,'tensor'=4] {'tensor'}, use_global_device_ids=true, to_apply=%region_30.31.clone | all-reduce | flops 4608 | bytes 18432
  598.0 40.0 %all-reduce.1 = (f32[192]{0:T(256)}, f32[192]{0:T(256)}, f32[6,192]{1,0:T(8,128)S(1)}, f32[768]{0:T(1024)}) all-reduce(f32[192]{0:T(256)S(1)} %get-tuple-element.259, f32[192]{0:T(256)S(1)} %get-tuple-element.258, f32[6,192]{1,0:T(8,128)S(1)} %reshape.391, f32[768]{0:T(1024)S(1)} %copy-done.30), channel_id=1, replica_groups=mesh['dp'=8,'tensor'=4] {'dp'}, use_global_device_ids=true, to_apply=%region_21.22 | all-reduce | flops 2304 | bytes 18432 | tf_op jit(solution)/shard_map/psum | solution.py:259
  638.6 174.0 %all-reduce.5.cloned.1.call-done = (f32[768,576]{0,1:T(8,128)}, f32[192,768]{1,0:T(8,128)}, f32[768,768]{1,0:T(8,128)}, f32[768,768]{1,0:T(8,128)}) async-done(((f32[768,576]{0,1:T(8,128)}, f32[192,768]{1,0:T(8,128)}, f32[768,768]{1,0:T(8,128)}, f32[768,768]{1,0:T(8,128)}), (f32[768,576]{0,1:T(8,128)}, f32[192,768]{1,0:T(8,128)}, f32[768,768]{1,0:T(8,128)}, ...) | async-done | bytes 7077904 | tf_op jit(solution)/shard_map/psum | solution.py:259
  815.4 41.7 %reduce-scatter.11.cloned.1.call-done = bf16[640,768]{1,0:T(8,128)(2,1)} async-done(((bf16[2560,768]{1,0:T(8,128)(2,1)}), bf16[640,768]{1,0:T(8,128)(2,1)}) %reduce-scatter.11.cloned.1.call-update) | async-done | bytes 983056 | tf_op jit(solution)/shard_map/reduce_scatter | solution.py:241
  (290 shorter events, 193.3 us)
Async XLA Ops:
  7.2 242.9 %copy-start = (bf16[768,768]{1,0:T(8,128)(2,1)S(1)}, bf16[768,768]{1,0:T(8,128)(2,1)}, u32[]{:S(2)}) copy-start(bf16[768,768]{1,0:T(8,128)(2,1)} %param.35) | copy-start | bytes 3538948
  7.2 38.1 %all-gather.4.cloned.1.call-start = ((), (), s32[]{:S(2)}) async-start(), calls=%async_computation.4 | async-start | bytes 4915200 | tf_op jit(solution)/shard_map/all_gather | solution.py:129
  7.9 167.4 %reduce-scatter.5.cloned.1.call-start = ((), (), s32[]{:S(2)}) async-start(), calls=%async_computation.5 | async-start | bytes 9830400 | tf_op jit(solution)/shard_map/reduce_scatter | solution.py:147
  11.7 38.3 %copy-start.19 = (bf16[768,576]{0,1:T(8,128)(2,1)}, bf16[768,576]{0,1:T(8,128)(2,1)S(1)}, u32[]{:S(2)}) copy-start(bf16[768,576]{0,1:T(8,128)(2,1)S(1)} %constant_dynamic-update-slice_fusion.1) | copy-start | bytes 2654212
  11.7 39.3 %copy-start.33 = (f32[192]{0:T(256)S(1)}, f32[192]{0:T(256)}, u32[]{:S(2)}) copy-start(f32[192]{0:T(256)} %param.27) | copy-start | bytes 2308
  11.7 39.3 %copy-start.34 = (f32[192]{0:T(256)S(1)}, f32[192]{0:T(256)}, u32[]{:S(2)}) copy-start(f32[192]{0:T(256)} %param.30) | copy-start | bytes 2308
  60.1 41.8 %copy-start.18 = (bf16[192,768]{1,0:T(8,128)(2,1)S(1)}, bf16[192,768]{1,0:T(8,128)(2,1)}, u32[]{:S(2)}) copy-start(bf16[192,768]{1,0:T(8,128)(2,1)} %param.31) | copy-start | bytes 884740
  101.9 4.2 copy-start.8
  106.1 69.2 %copy-start.29 = (f32[768]{0:T(1024)S(1)}, f32[768]{0:T(1024)}, u32[]{:S(2)}) copy-start(f32[768]{0:T(1024)} %param.32) | copy-start | bytes 9220
  106.2 71.6 %copy-start.21 = (f32[768]{0:T(1024)S(1)}, f32[768]{0:T(1024)}, u32[]{:S(2)}) copy-start(f32[768]{0:T(1024)} %param.33) | copy-start | bytes 9220
  106.2 71.6 %copy-start.31 = (f32[768]{0:T(1024)S(1)}, f32[768]{0:T(1024)}, u32[]{:S(2)}) copy-start(f32[768]{0:T(1024)} %param.34) | copy-start | bytes 9220
  106.2 202.9 %reduce-scatter.7.cloned.1.call-start = ((), (), s32[]{:S(2)}) async-start(), calls=%async_computation.6 | async-start | bytes 4915200 | tf_op jit(solution)/shard_map/reduce_scatter | solution.py:169
  179.6 12.4 %collective-permute-start = (bf16[640,768]{1,0:T(8,128)(2,1)}, bf16[640,768]{1,0:T(8,128)(2,1)S(1)}, u32[]{:S(2)}, u32[]{:S(2)}) collective-permute-start(bf16[640,768]{1,0:T(8,128)(2,1)} %get-tuple-element.234), channel_id=1, source_target_pairs={{0,3},{1,0},{2,1},{3,2},{4,7},{5,4},{6,5},{7,6},{8,11},{9,8},{10,9... | collective-permute-start | bytes 2949128 | tf_op jit(solution)/shard_map/ppermute | solution.py:161
  195.5 45.4 %collective-permute-start.1 = (bf16[1280,768]{1,0:T(8,128)(2,1)}, bf16[1280,768]{1,0:T(8,128)(2,1)}, u32[]{:S(2)}, u32[]{:S(2)}) collective-permute-start(bf16[1280,768]{1,0:T(8,128)(2,1)} %pad_maximum_fusion), channel_id=1, source_target_pairs={{0,2},{1,3},{2,0},{3,1},{4,6},{5,7},{6,4},{7,5},{8,10},{9,11},{10,... | collective-permute-start | bytes 5898248 | tf_op jit(solution)/shard_map/ppermute | solution.py:161
  199.2 46.9 %copy-start.6 = (bf16[640,768]{1,0:T(8,128)(2,1)S(1)}, bf16[640,768]{1,0:T(8,128)(2,1)}, u32[]{:S(2)}) copy-start(bf16[640,768]{1,0:T(8,128)(2,1)} %copy-done.5) | copy-start | bytes 2949124
  250.1 9.8 %copy-start.36 = (bf16[768,768]{1,0:T(8,128)(2,1)S(1)}, bf16[768,768]{1,0:T(8,128)(2,1)}, u32[]{:S(2)}) copy-start(bf16[768,768]{1,0:T(8,128)(2,1)} %param.37) | copy-start | bytes 3538948
  264.7 44.3 %copy-start.20 = (f32[768]{0:T(1024)S(1)}, f32[768]{0:T(1024)}, u32[]{:S(2)}) copy-start(f32[768]{0:T(1024)} %param.38) | copy-start | bytes 9220
  264.7 48.4 %copy-start.22 = (f32[768]{0:T(1024)S(1)}, f32[768]{0:T(1024)}, u32[]{:S(2)}) copy-start(f32[768]{0:T(1024)} %param.39) | copy-start | bytes 9220
  264.7 48.4 %copy-start.32 = (f32[768]{0:T(1024)S(1)}, f32[768]{0:T(1024)}, u32[]{:S(2)}) copy-start(f32[768]{0:T(1024)} %param.40) | copy-start | bytes 9220
  264.7 89.2 %all-gather.6.cloned.1.call-start = ((), (), s32[]{:S(2)}) async-start(), calls=%async_computation.7 | async-start | bytes 4915200 | tf_op jit(solution)/shard_map/all_gather | solution.py:184
  309.0 4.1 copy-start.12
  320.8 92.5 %reduce-scatter.9.cloned.1.call-start = ((), (), s32[]{:S(2)}) async-start(), calls=%async_computation.8 | async-start | bytes 4915200 | tf_op jit(solution)/shard_map/reduce_scatter | solution.py:191
  370.3 82.6 %all-gather.8.cloned.1.call-start = ((), (), s32[]{:S(2)}) async-start(), calls=%async_computation.9 | async-start | bytes 4915200 | tf_op jit(solution)/shard_map/all_gather | solution.py:204
  419.7 393.0 %all-reduce.5.cloned.1.call-start = ((), (), s32[]{:S(2)}) async-start(), calls=%async_computation.11 | async-start | bytes 14155776 | tf_op jit(solution)/shard_map/psum | solution.py:259
  419.7 8.2 copy-start.35
  419.7 8.2 copy-start.40
  561.2 4.8 copy-start.9
  576.1 281.0 %reduce-scatter.11.cloned.1.call-start = ((), (), s32[]{:S(2)}) async-start(), calls=%async_computation.10 | async-start | bytes 4915200 | tf_op jit(solution)/shard_map/reduce_scatter | solution.py:241
  583.9 13.7 %copy-start.4 = (bf16[5,512,576]{1,2,0:T(8,128)(2,1)S(1)}, bf16[5,512,576]{1,2,0:T(8,128)(2,1)}, u32[]{:S(2)}) copy-start(bf16[5,512,576]{1,2,0:T(8,128)(2,1)} %get-tuple-element.109) | copy-start | bytes 8847364
  583.9 14.2 %copy-start.30 = (f32[768]{0:T(1024)S(1)}, f32[768]{0:T(1024)}, u32[]{:S(2)}) copy-start(f32[768]{0:T(1024)} %get-tuple-element.262) | copy-start | bytes 9220
  598.0 259.1 %copy-start.7 = (f32[640,768]{1,0:T(8,128)S(1)}, f32[640,768]{1,0:T(8,128)}, u32[]{:S(2)}) copy-start(f32[640,768]{1,0:T(8,128)} %get-tuple-element.232) | copy-start | bytes 5898244
  812.6 47.0 %copy-start.17 = (f32[192,768]{1,0:T(8,128)S(1)}, f32[192,768]{1,0:T(8,128)}, u32[]{:S(2)}) copy-start(f32[192,768]{1,0:T(8,128)} %get-tuple-element.450) | copy-start | bytes 1769476
  (24 other events, 50.8 us)
Sparse Core Ops, SparseCore 0:
  9.6 35.6 all-gather.3
  106.3 68.9 reduce-scatter.4
  264.9 44.1 reduce-scatter.6
  320.9 32.9 all-gather.5
  370.4 42.8 reduce-scatter.8
  419.8 33.0 all-gather.7
  576.2 236.3 all-reduce.4
  815.2 41.8 reduce-scatter.10
